TPU v7x, 32 devices: a whole 2x2x4 slice. The times are simulated.
32 devices in a mesh: ctx: 8 (over y, x, core), exp: 4 (over z).
Axes of the slice: x: 2, y: 2, z: 4, core: 2. Of those that a mesh axis runs over, the one named last changes fastest.
Arguments:
- mixer_input: bfloat16 [8192, 4096], P('ctx', 'exp'), may hold values from -6 to 6
- scale_exponent: int32 [64, 64], P('ctx', 'exp'), may hold values from -1 to 1
- step_size: float32 [64, 8192], P('exp', 'ctx'), may hold values from 0.25 to 1
- decay_log: float32 [64, 8192], P('exp', 'ctx'), may hold values from -1.2 to 0
- state_input: bfloat16 [8192, 128], P('ctx'), may hold values from -6 to 6
- state_output: bfloat16 [8192, 128], P('ctx'), may hold values from -0.5 to 0.5
- skip_gain: float32 [64], P('exp'), may hold values from 0.5 to 1.5
- gate_input: bfloat16 [8192, 4096], P('ctx', 'exp'), may hold values from -6 to 6
- norm_gain: float32 [4096], P('exp'), may hold values from 0.25 to 1.75
- up_weight: bfloat16 [4096, 3072], P('ctx', 'exp'), may hold values from -0.09375 to 0.09375
- down_weight: bfloat16 [3072, 4096], P('exp', 'ctx'), may hold values from -0.15625 to 0.15625
- expert_slot: int32 [8192], P('ctx'), may hold values from 0 to 256, as said below
- gate_prob: float32 [8192], P('ctx'), may hold values from 0.2 to 1
Outputs:
- layer_out: bfloat16 [8192, 4096], P('ctx', 'exp')
Inputs may be any that keep to these rules, and one draw needn't show every extreme that they name: `expert_slot`: within each aligned block of 1024 tokens, the tokens routed to the expert carry the distinct slots 0 to k - 1 for some k of at most 256, and all other tokens carry 256; in some block k equals 256.
All inputs are finite; a program needn't handle non-finite values.
Results may differ from a plain program's by a relative error of at most 0.0085.
Values may be sent and summed in bfloat16 or wider, within the bound.
No kernel may reach another device: no remote copies, remote signals or barrier semaphores. Data moves between devices by JAX's collectives and lax.ppermute only.
A program may use at most 128 MiB of HBM per device.

v0:
```python
import jax
import jax.numpy as jnp
from jax import lax
from jax.sharding import PartitionSpec as P

P_SIZE = 64
BLK = 128
CAP = 256
highest = lax.Precision.HIGHEST


def local_scan(x_in, step_size, decay_log, b_rows, c_rows):
    length, head_count, head_width = x_in.shape
    blocks = length // BLK
    x_blocks = x_in.reshape(blocks, BLK, head_count, head_width)
    b_blocks = b_rows.reshape(blocks, BLK, b_rows.shape[1])
    c_blocks = c_rows.reshape(blocks, BLK, c_rows.shape[1])
    step_blocks = step_size.reshape(head_count, blocks, BLK)
    cumulative = jnp.cumsum(decay_log.reshape(head_count, blocks, BLK), axis=2)
    scores = jnp.einsum("bin,bjn->bij", c_blocks, b_blocks, precision=highest)
    causal = jnp.arange(BLK)[:, None] >= jnp.arange(BLK)[None, :]
    spread = jnp.where(causal, cumulative[:, :, :, None] - cumulative[:, :, None, :], -jnp.inf)
    mixing = jnp.exp(spread) * scores[None] * step_blocks[:, :, None, :]
    inner_part = jnp.einsum("hbij,bjhp->bihp", mixing, x_blocks, precision=highest)
    tail_decay = jnp.exp(cumulative[:, :, -1:] - cumulative) * step_blocks
    block_state = jnp.einsum(
        "hbj,bjn,bjhp->bhnp", tail_decay, b_blocks, x_blocks, precision=highest
    )
    totals = cumulative[:, :, -1]

    def carry_on(running, block_items):
        block_total, block_end = block_items
        return (jnp.exp(block_total)[:, None, None] * running + block_end, running)

    running, entering = lax.scan(
        carry_on, jnp.zeros(block_state.shape[1:], jnp.float32), (totals.T, block_state)
    )
    carried = jnp.einsum(
        "bin,hbi,bhnp->bihp", c_blocks, jnp.exp(cumulative), entering, precision=highest
    )
    offsets = jnp.cumsum(totals, axis=1) - totals
    growth = jnp.exp(offsets[:, :, None] + cumulative)
    return (inner_part + carried, running, jnp.sum(totals, axis=1), c_blocks, growth)


def body(
    mixer_input,
    scale_exponent,
    step_size,
    decay_log,
    state_input,
    state_output,
    skip_gain,
    gate_input,
    norm_gain,
    up_weight,
    down_weight,
    expert_slot,
    gate_prob,
):
    length = mixer_input.shape[0]
    head_count = skip_gain.shape[0]
    blocks = length // BLK
    factor = jnp.exp2(scale_exponent.astype(jnp.float32))
    x_in = (
        mixer_input.astype(jnp.float32).reshape(blocks, BLK, head_count, P_SIZE)
        * factor[:, None, :, None]
    ).reshape(length, head_count, P_SIZE)
    b_rows = state_input.astype(jnp.float32)
    c_rows = state_output.astype(jnp.float32)
    local_out, end_state, total_log, c_blocks, growth = local_scan(
        x_in, step_size, decay_log, b_rows, c_rows
    )
    log_totals = lax.all_gather(total_log[None, :], "ctx", axis=0, tiled=True)
    before = jnp.cumsum(log_totals, axis=0) - log_totals
    position = lax.axis_index("ctx")
    own_prior = lax.dynamic_index_in_dim(before, position, 0, keepdims=False)
    shard_piece = lax.all_gather(
        end_state[None].astype(jnp.bfloat16), "ctx", axis=0, tiled=True
    ).astype(jnp.float32)
    row_count = shard_piece.shape[0]
    row_ids = jnp.arange(row_count, dtype=jnp.int32)
    decay_gap = jnp.minimum(own_prior[None, :] - before - log_totals, 0.0)
    weight = jnp.where((row_ids < position)[:, None], jnp.exp(decay_gap), 0.0)
    start_state = jnp.zeros_like(end_state) + jnp.einsum(
        "kh,khnp->hnp", weight, shard_piece, precision=highest
    )
    handed = jnp.einsum("bin,hbi,hnp->bihp", c_blocks, growth, start_state, precision=highest)
    mixer_out = (local_out + handed).reshape(length, head_count, P_SIZE) + skip_gain[
        None, :, None
    ] * x_in
    gated_out = mixer_out * jax.nn.silu(
        gate_input.astype(jnp.float32).reshape(length, head_count, P_SIZE)
    )
    inverse_rms = lax.rsqrt(jnp.mean(gated_out * gated_out, axis=2, keepdims=True) + 1e-05)
    normed = (
        (gated_out * inverse_rms * norm_gain.reshape(head_count, P_SIZE))
        .reshape(length, head_count * P_SIZE)
        .astype(jnp.bfloat16)
    )
    places = jnp.arange(CAP, dtype=jnp.int32)[:, None] == expert_slot[None, :]
    picker = places.astype(jnp.bfloat16)
    dispatched = jnp.dot(picker, normed, preferred_element_type=jnp.float32).astype(jnp.bfloat16)
    full_features = lax.all_gather(dispatched, "exp", axis=1, tiled=True)
    up_act = jnp.dot(
        full_features,
        lax.all_gather(up_weight, "ctx", axis=0, tiled=True),
        preferred_element_type=jnp.float32,
    )
    hidden = jax.nn.silu(up_act).astype(jnp.bfloat16)
    terms = jnp.dot(
        hidden,
        lax.all_gather(down_weight, "ctx", axis=1, tiled=True),
        preferred_element_type=jnp.float32,
    )
    own_sums = lax.psum_scatter(
        terms.astype(jnp.bfloat16), "exp", scatter_dimension=1, tiled=True
    ).astype(jnp.float32)
    selector = places.astype(jnp.float32)
    expert_tok = lax.dot_general(selector, own_sums, (((0,), (0,)), ((), ())), precision=highest)
    return (normed.astype(jnp.float32) + gate_prob[:, None] * expert_tok).astype(jnp.bfloat16)


def solution(mesh):
    in_specs = (
        P("ctx", "exp"),
        P("ctx", "exp"),
        P("exp", "ctx"),
        P("exp", "ctx"),
        P("ctx", None),
        P("ctx", None),
        P("exp"),
        P("ctx", "exp"),
        P("exp"),
        P("ctx", "exp"),
        P("exp", "ctx"),
        P("ctx"),
        P("ctx"),
    )
    out_specs = P("ctx", "exp")
    return jax.shard_map(body, mesh=mesh, in_specs=in_specs, out_specs=out_specs, check_vma=False)
```

profile of v0, /device:TPU:0, one launch (start us, length us, event | category | flops | bytes accessed | tf_op | source)
XLA Modules:
  0.0 375.8 jit_solution(6003521538814983370)
XLA Ops:
  7.4 4.5 %reduce_window_sum.33 = f32[16,8,128]{2,1,0:T(8,128)S(1)} reduce-window(f32[16,8,128]{2,1,0:T(8,128)S(1)} %bitcast.107, f32[]{:T(128)} %constant.28.clone.1), window={size=1x1x128 pad=0_0x0_0x127_0}, to_apply=%region_0.0 | reduce-window | flops 2080768 | bytes 131076 | tf_op jit(solution)/shard_map/jit(cumsum)/reduce_window_sum | solution.py:19
  14.6 6.8 %reshape.91 = f32[8,128,16,64]{3,2,1,0:T(8,128)} reshape(bf16[1024,1024]{1,0:T(8,128)(2,1)} %param.15) | data formatting | bytes 6291456 | tf_op jit(solution)/shard_map/reshape | solution.py:66
  21.4 7.2 %copy.74 = f32[8,128,16,64]{1,3,2,0:T(8,128)} copy(f32[8,128,16,64]{3,2,1,0:T(8,128)} %reshape.91) | data formatting | bytes 8388608 | tf_op jit(solution)/shard_map/reshape | solution.py:66
  28.5 6.4 %fusion.20 = f32[8,16,128,64]{2,3,1,0:T(8,128)} fusion(bf16[8,128,128,1]{2,1,3,0:T(8,128)(2,1)S(1)} %bitcast.102, f32[8,128,16,64]{1,3,2,0:T(8,128)} %copy.74, f32[8,128,16]{1,2,0:T(8,128)S(1)} %copy.81, f32[8,16]{1,0:T(8,128)S(1)} %multiply_exponential_fusion), kind=kOutput, calls=%fused_computation.31 | convolution fusion | flops 1612709888 | bytes 8716800 | tf_op jit(solution)/shard_map/hbj,bjn,bjhp->bhnp/dot_general | solution.py:26
  35.0 21.8 %while.13 = (s32[]{:T(128)}, f32[16,128,64]{2,1,0:T(8,128)S(1)}, f32[8,16,128,64]{3,2,1,0:T(8,128)}, f32[8,16]{1,0:T(8,128)S(1)}, f32[8,16,128,64]{2,3,1,0:T(8,128)}, /*index=5*/s32[]{:T(128)}, s32[]{:T(128)}) while((s32[]{:T(128)}, f32[16,128,64]{2,1,0:T(8,128)S(1)}, f32[8,16,128,64]{3,2,1,0:T(8,128)}, f32[8,16]{1,0:T(8,128)S(1)}, ...), condition=%wide.region_2.3_spmd.clone, body=%wide.region_1.2_spmd.clone.sunk | while | flops 524291 | bytes 5243680 | solution.py:35
  59.4 15.6 %all-reduce = f32[128]{0:T(128)S(1)} all-reduce(f32[128]{0:T(128)S(1)} %dynamic-update-slice), channel_id=2, replica_groups=mesh['ctx'=8,'exp'=4] {'ctx'}, use_global_device_ids=true, to_apply=%add | all-reduce | flops 128 | bytes 1024
  75.1 6.8 %reshape.93 = f32[8,128,16,64]{3,2,1,0:T(8,128)} reshape(bf16[1024,1024]{1,0:T(8,128)(2,1)} %param.22) | data formatting | bytes 6291456 | tf_op jit(solution)/shard_map/reshape | solution.py:93
  81.9 7.2 %copy.94 = f32[8,128,16,64]{1,3,2,0:T(8,128)} copy(f32[8,128,16,64]{3,2,1,0:T(8,128)} %reshape.93) | data formatting | bytes 8388608 | tf_op jit(solution)/shard_map/reshape | solution.py:93
  89.2 2.5 mul.135
  91.6 5.4 %copy.90 = f32[1024,1024]{1,0:T(8,128)} copy(f32[1024,1024]{0,1:T(8,128)} %bitcast.99) | data formatting | bytes 8388608 | tf_op jit(solution)/shard_map/mul | solution.py:66
  97.6 12.1 %fusion.35 = f32[8,16,64,128]{3,2,1,0:T(8,128)} fusion(f32[8,16,128,64]{3,2,1,0:T(8,128)} %get-tuple-element.33, bf16[8,128,128,1]{2,1,3,0:T(8,128)(2,1)S(1)} %bitcast.96), kind=kOutput, calls=%fused_computation.60 | convolution fusion | flops 1610612736 | bytes 8650752 | tf_op jit(solution)/shard_map/bin,hbi,bhnp->bihp/dot_general | solution.py:38
  109.8 18.0 %fusion.2 = f32[8,16,64,128]{3,2,1,0:T(8,128)} fusion(f32[16,8,128]{2,0,1:T(8,128)S(1)} %copy_bitcast_fusion.2, f32[8,128,128]{2,1,0:T(8,128)S(1)} %fusion.34, f32[16,8,128]{2,0,1:T(8,128)S(1)} %copy.75, pred[128,128]{1,0:T(8,128)(4,1)S(1)} %iota_compare_fusion.3, f32[8,128,16,64]{1,3,2,0:T(8,128)S(1)} %copy-done.2, f32[8,16]{1,0:T(8,128)S(1)} %multiply_exponential_fusion), kind=kOutput, calls=%fused_computation.6 | convolution fusion | flops 1620049920 | bytes 9060864 | tf_op jit(solution)/shard_map/hbij,bjhp->bihp/dot_general | solution.py:24
  129.8 9.3 %multiply_reduce_fusion.1 = (f32[8,128,16]{1,2,0:T(8,128)S(1)}, f32[8,128,16,64]{1,3,2,0:T(8,128)}) fusion(f32[8,128,16,64]{1,3,2,0:T(8,128)} %copy.94, f32[8,128,16,64]{1,3,2,0:T(8,128)} %copy.74, f32[16]{0:T(128)S(1)} %copy-done.9, f32[8,16]{1,0:T(8,128)S(1)} %multiply_exponential_fusion, bf16[8,128,128,1]{2,1,3,0:T(8,128)(2,1)S(1)} %bitcast.97, ...), kind=kOutput, calls=%fused_computation.20 | convolution fusion | flops 1625276416 | bytes 21955136 | tf_op jit(solution)/shard_map/bin,hbi,hnp->bihp/dot_general | solution.py:88
  139.1 7.1 %copy.110 = f32[8,128,16,64]{3,2,1,0:T(8,128)} copy(f32[8,128,16,64]{1,3,2,0:T(8,128)} %get-tuple-element.89) | data formatting | bytes 8388608 | tf_op jit(solution)/shard_map/reshape | solution.py:89
  146.3 7.6 %reshape.92 = f32[1024,1024]{1,0:T(8,128)} reshape(f32[8,128,16,64]{3,2,1,0:T(8,128)} %copy.110) | data formatting | bytes 8388608 | tf_op jit(solution)/shard_map/reshape | solution.py:89
  153.9 2.5 mul.146
  156.4 5.5 %copy.96 = f32[1024,1024]{1,0:T(8,128)} copy(f32[1024,1024]{0,1:T(8,128)} %bitcast.100) | data formatting | bytes 8388608 | tf_op jit(solution)/shard_map/mul | solution.py:97
  161.9 6.6 %multiply_convert_fusion = bf16[1024,1024]{1,0:T(8,128)(2,1)S(1)} fusion(f32[1024,1024]{1,0:T(8,128)} %copy.96, f32[1024,1024]{1,0:T(8,128)} %reshape.92, f32[1024,1024]{1,0:T(8,128)} %copy.90, f32[1024]{0:T(1024)S(1)} %copy-done.8, f32[1024]{0:T(1024)S(1)} %mul.131, bf16[1024,1024]{1,0:T(8,128)(2,1)S(1)} %copy-done.3, bf16[1024,1024]{1,0:T(8,128)(2,1)} %param.15), kind=kLoop, calls=%fused_computation.19 | loop fusion | flops 13631488 | bytes 18882560 | tf_op jit(solution)/shard_map/convert_element_type | solution.py:99
  172.8 43.8 %all-gather.7.cloned.1.call-done = bf16[256,4096]{1,0:T(8,128)(2,1)} async-done(((bf16[256,1024]{1,0:T(8,128)(2,1)}), bf16[256,4096]{1,0:T(8,128)(2,1)}) %all-gather.7.cloned.1.call-update) | async-done | bytes 2097168 | tf_op jit(solution)/shard_map/all_gather | solution.py:104
  216.6 47.3 %all-gather.11.cloned.1.call-done = bf16[768,4096]{1,0:T(8,128)(2,1)} async-done(((bf16[768,512]{1,0:T(8,128)(2,1)}), bf16[768,4096]{1,0:T(8,128)(2,1)}) %all-gather.11.cloned.1.call-update) | async-done | bytes 6291472 | tf_op jit(solution)/shard_map/all_gather | solution.py:113
  263.9 47.2 %all-gather.9.cloned.1.call-done = bf16[4096,768]{1,0:T(8,128)(2,1)} async-done(((bf16[512,768]{1,0:T(8,128)(2,1)}), bf16[4096,768]{1,0:T(8,128)(2,1)}) %all-gather.9.cloned.1.call-update) | async-done | bytes 6291472 | tf_op jit(solution)/shard_map/all_gather | solution.py:107
  311.1 11.1 %convolution_convert_fusion = bf16[256,4096]{1,0:T(8,128)(2,1)} fusion(bf16[768,4096]{1,0:T(8,128)(2,1)} %all-gather.11.cloned.1.call-done, bf16[256,4096]{1,0:T(8,128)(2,1)} %all-gather.7.cloned.1.call-done, bf16[4096,768]{1,0:T(8,128)(2,1)} %all-gather.9.cloned.1.call-done), kind=kOutput, calls=%fused_computation.12 | convolution fusion | flops 3223257088 | bytes 16777216 | tf_op jit(solution)/shard_map/dot_general | solution.py:111
  322.2 43.8 %reduce-scatter.2.cloned.1.call-done = bf16[256,1024]{1,0:T(8,128)(2,1)} async-done(((bf16[256,4096]{1,0:T(8,128)(2,1)}), bf16[256,1024]{1,0:T(8,128)(2,1)}) %reduce-scatter.2.cloned.1.call-update) | async-done | bytes 524304 | tf_op jit(solution)/shard_map/reduce_scatter | solution.py:116
  366.0 3.3 add_convert_fusion
  (114 shorter events, 34.0 us)
Async XLA Ops:
  6.5 90.8 %copy-start = (bf16[1024,128]{1,0:T(8,128)(2,1)S(1)}, bf16[1024,128]{1,0:T(8,128)(2,1)}, u32[]{:S(2)}) copy-start(bf16[1024,128]{1,0:T(8,128)(2,1)} %param.20) | copy-start | bytes 786436
  6.5 121.2 %all-gather.13.cloned.1.call-start = ((), (), s32[]{:S(2)}) async-start(), calls=%async_computation.5 | async-start | bytes 2359296 | tf_op jit(solution)/shard_map/all_gather | solution.py:78
  21.4 7.2 %copy-start.6 = (bf16[1024,128]{1,0:T(8,128)(2,1)S(1)}, bf16[1024,128]{1,0:T(8,128)(2,1)}, u32[]{:S(2)}) copy-start(bf16[1024,128]{1,0:T(8,128)(2,1)} %param.19) | copy-start | bytes 786436
  35.0 22.9 %copy-start.12 = (u32[32]{0:T(128)S(1)}, u32[32]{0:T(128)}, u32[]{:S(2)}) copy-start(u32[32]{0:T(128)} %constant.54) | copy-start | bytes 388
  57.7 158.9 %all-gather.7.cloned.1.call-start = ((), (), s32[]{:S(2)}) async-start(), calls=%async_computation.1 | async-start | bytes 2621440 | tf_op jit(solution)/shard_map/all_gather | solution.py:104
  91.6 5.4 %copy-start.9 = (f32[16]{0:T(128)S(1)}, f32[16]{0:T(128)}, u32[]{:S(2)}) copy-start(f32[16]{0:T(128)} %param.21) | copy-start | bytes 196
  91.6 5.7 %copy-start.7 = (f32[16,1024]{1,0:T(8,128)S(1)}, f32[16,1024]{1,0:T(8,128)}, u32[]{:S(2)}) copy-start(f32[16,1024]{1,0:T(8,128)} %param.17) | copy-start | bytes 196612
  97.6 12.1 %copy-start.2 = (f32[8,128,16,64]{1,3,2,0:T(8,128)S(1)}, f32[8,128,16,64]{1,3,2,0:T(8,128)}, u32[]{:S(2)}) copy-start(f32[8,128,16,64]{1,3,2,0:T(8,128)} %copy.74) | copy-start | bytes 12582916
  156.4 5.5 %copy-start.3 = (bf16[1024,1024]{1,0:T(8,128)(2,1)S(1)}, bf16[1024,1024]{1,0:T(8,128)(2,1)}, u32[]{:S(2)}) copy-start(bf16[1024,1024]{1,0:T(8,128)(2,1)} %param.22) | copy-start | bytes 6291460
  156.4 5.5 %copy-start.8 = (f32[1024]{0:T(1024)S(1)}, f32[1024]{0:T(1024)}, u32[]{:S(2)}) copy-start(f32[1024]{0:T(1024)} %param.23) | copy-start | bytes 12292
  161.9 7.9 %copy-start.10 = (s32[1024]{0:T(1024)S(1)}, s32[1024]{0:T(1024)}, u32[]{:S(2)}) copy-start(s32[1024]{0:T(1024)} %param.26) | copy-start | bytes 12292
  168.5 1.3 copy-start.4
  171.4 92.5 %all-gather.11.cloned.1.call-start = ((), (), s32[]{:S(2)}) async-start(), calls=%async_computation.3 | async-start | bytes 7077888 | tf_op jit(solution)/shard_map/all_gather | solution.py:113
  172.2 138.9 %all-gather.9.cloned.1.call-start = ((), (), s32[]{:S(2)}) async-start(), calls=%async_computation.2 | async-start | bytes 7077888 | tf_op jit(solution)/shard_map/all_gather | solution.py:107
  172.7 193.2 %copy-start.5 = (bf16[1024,1024]{1,0:T(8,128)(2,1)S(1)}, bf16[1024,1024]{1,0:T(8,128)(2,1)}, u32[]{:S(2)}) copy-start(bf16[1024,1024]{1,0:T(8,128)(2,1)} %copy-done.4) | copy-start | bytes 6291460
  172.8 193.2 %copy-start.11 = (f32[1024]{0:T(1024)S(1)}, f32[1024]{0:T(1024)}, u32[]{:S(2)}) copy-start(f32[1024]{0:T(1024)} %param.27) | copy-start | bytes 12292
  172.8 193.2 %reduce-scatter.2.cloned.1.call-start = ((), (), s32[]{:S(2)}) async-start(), calls=%async_computation.4 | async-start | bytes 2621440 | tf_op jit(solution)/shard_map/reduce_scatter | solution.py:116
  311.1 58.2 %copy-start.1 = (bf16[1024,128]{1,0:T(8,128)(2,1)S(1)}, bf16[1024,128]{1,0:T(8,128)(2,1)}, u32[]{:S(2)}) copy-start(bf16[1024,128]{1,0:T(8,128)(2,1)} %param.20) | copy-start | bytes 786436
Sparse Core Ops, SparseCore 0:
  57.8 30.5 all-gather.12
  171.5 45.0 all-gather.6
  218.5 45.3 all-gather.10
  265.6 45.3 all-gather.8
  322.3 43.6 reduce-scatter.1
where the time goes:
time: 377 us; the launch traced here: 376 us
  waiting for transfers between devices  183 us (49%)
  local copies, waits for them, and re-layouts  75.8 us (20%)
  matrix products  62 us (16%)
  other arithmetic  24.6 us (7%)
  blocking collectives  15.6 us (4%)
  between operations  14 us (4%)
    all_gather x1, waiting for transfers between devices, body(): lax.all_gather(down_weight, 'ctx', axis=1, tiled=True)  47.3 us
    all_gather x1, waiting for transfers between devices, body(): lax.all_gather(up_weight, 'ctx', axis=0, tiled=True)  47.2 us
    all_gather x1, waiting for transfers between devices, body(): full_features = lax.all_gather(dispatched, 'exp', axis=1, tiled=True)  43.8 us
    reduce_scatter x1, waiting for transfers between devices, body(): lax.psum_scatter(terms.astype(jnp.bfloat16), 'exp', scatter_dimension=1,...  43.8 us
    dot_general x1, matrix products, local_scan(): jnp.einsum('hbij,bjhp->bihp', mixing, x_blocks, precision=highest)  18 us
    unnamed x1, blocking collectives  15.6 us
    reshape x2, local copies, waits for them, and re-layouts, body(): (local_out + handed).reshape(length, head_count, P_SIZE)  14.8 us
    reshape x2, local copies, waits for them, and re-layouts, body(): gate_input.astype(jnp.float32).reshape(length, head_count, P_SIZE)  14 us
  transfers between devices with their start and end apart: 5, of which 4 were waited for; matrix products, arithmetic and copies ran while one was open for 14% of the time, Pallas kernels for 0%

commit v1 on v0

--- a/solution.py
+++ b/solution.py
@@ -101,7 +101,15 @@
     places = jnp.arange(CAP, dtype=jnp.int32)[:, None] == expert_slot[None, :]
     picker = places.astype(jnp.bfloat16)
     dispatched = jnp.dot(picker, normed, preferred_element_type=jnp.float32).astype(jnp.bfloat16)
-    full_features = lax.all_gather(dispatched, "exp", axis=1, tiled=True)
+    num = lax.axis_size("exp")
+    seen = [dispatched]
+    m = 0
+    while m < num - 1:
+        seen.append(lax.ppermute(seen[-1], "exp", [(j0, (j0 + 1) % num) for j0 in range(num)]))
+        m = m + 1
+    full_features = jnp.roll(
+        jnp.concatenate(seen[::-1], 1), (lax.axis_index("exp") + 1) * dispatched.shape[1], 1
+    )
     up_act = jnp.dot(
         full_features,
         lax.all_gather(up_weight, "ctx", axis=0, tiled=True),

time: 377 us -> 287 us (0.76)
  waiting for transfers between devices: 183 us -> 85.4 us
  local copies, waits for them, and re-layouts: 75.8 us -> 81.3 us
    all_gather x1, waiting for transfers between devices: 47.3 us -> 0.01 us  [body(): lax.all_gather(down_weight, 'ctx', axis=1, tiled=True)]
    all_gather x1, waiting for transfers between devices: 47.2 us -> 0.01 us  [body(): lax.all_gather(up_weight, 'ctx', axis=0, tiled=True)]
    all_gather x1 -> x0, waiting for transfers between devices: 43.8 us -> none  [body(): full_features = lax.all_gather(dispatched, 'exp', axis=1, tiled=True)]
    ppermute x0 -> x3, waiting for transfers between devices: none -> 39.4 us  [body(): lax.ppermute(seen[-1], 'exp', [(j0, (j0 + 1) % num) for j0 in range(num)])]
    unnamed x32 -> x41, local copies, waits for them, and re-layouts: 4.04 us -> 10.1 us
  transfers between devices with their start and end apart: 5 -> 7, of which waited for: 4 -> 4; matrix products, arithmetic and copies ran while one was open for 14% -> 36% of each run, Pallas kernels for 0% -> 0%
where the time goes in v1:
time: 287 us; the launch traced here: 286 us
  waiting for transfers between devices  85.4 us (30%)
  local copies, waits for them, and re-layouts  81.3 us (28%)
  matrix products  61.9 us (22%)
  other arithmetic  25.5 us (9%)
  blocking collectives  15.5 us (5%)
  between operations  14 us (5%)
    reduce_scatter x1, waiting for transfers between devices, body(): lax.psum_scatter(terms.astype(jnp.bfloat16), 'exp', scatter_dimension=1,...  44.6 us
    ppermute x3, waiting for transfers between devices, body(): lax.ppermute(seen[-1], 'exp', [(j0, (j0 + 1) % num) for j0 in range(num)])  39.4 us
    dot_general x1, matrix products, local_scan(): jnp.einsum('hbij,bjhp->bihp', mixing, x_blocks, precision=highest)  18 us
    unnamed x1, blocking collectives  15.5 us
    reshape x2, local copies, waits for them, and re-layouts, body(): (local_out + handed).reshape(length, head_count, P_SIZE)  14.9 us
    reshape x2, local copies, waits for them, and re-layouts, body(): mixer_input.astype(jnp.float32).reshape(blocks, BLK, head_count, P_SIZE)  14 us
    dot_general x1, matrix products, local_scan(): jnp.einsum('bin,hbi,bhnp->bihp', c_blocks, jnp.exp(cumulative), entering,...  12.5 us
    reshape x2, local copies, waits for them, and re-layouts, body(): gate_input.astype(jnp.float32).reshape(length, head_count, P_SIZE)  11.7 us
  transfers between devices with their start and end apart: 7, of which 4 were waited for; matrix products, arithmetic and copies ran while one was open for 36% of the time, Pallas kernels for 0%

profile of v1, /device:TPU:0, one launch (start us, length us, event | category | flops | bytes accessed | tf_op | source)
XLA Modules:
  0.0 285.8 jit_solution(8292433175519200548)
XLA Ops:
  7.4 4.5 %reduce_window_sum.33 = f32[16,8,128]{2,1,0:T(8,128)S(1)} reduce-window(f32[16,8,128]{2,1,0:T(8,128)S(1)} %bitcast.106, f32[]{:T(128)} %constant.65.clone.1), window={size=1x1x128 pad=0_0x0_0x127_0}, to_apply=%region_0.0 | reduce-window | flops 2080768 | bytes 131076 | tf_op jit(solution)/shard_map/jit(cumsum)/reduce_window_sum | solution.py:19
  15.1 6.8 %reshape.91 = f32[8,128,16,64]{3,2,1,0:T(8,128)} reshape(bf16[1024,1024]{1,0:T(8,128)(2,1)} %param.15) | data formatting | bytes 6291456 | tf_op jit(solution)/shard_map/reshape | solution.py:66
  21.9 7.1 %copy.74 = f32[8,128,16,64]{1,3,2,0:T(8,128)} copy(f32[8,128,16,64]{3,2,1,0:T(8,128)} %reshape.91) | data formatting | bytes 8388608 | tf_op jit(solution)/shard_map/reshape | solution.py:66
  29.1 6.4 %fusion.20 = f32[8,16,128,64]{2,3,1,0:T(8,128)} fusion(bf16[8,128,128,1]{2,1,3,0:T(8,128)(2,1)S(1)} %bitcast.101, f32[8,128,16,64]{1,3,2,0:T(8,128)} %copy.74, f32[8,128,16]{1,2,0:T(8,128)S(1)} %copy.81, f32[8,16]{1,0:T(8,128)S(1)} %multiply_exponential_fusion), kind=kOutput, calls=%fused_computation.31 | convolution fusion | flops 1612709888 | bytes 8716800 | tf_op jit(solution)/shard_map/hbj,bjn,bjhp->bhnp/dot_general | solution.py:26
  35.5 21.8 %while.13 = (s32[]{:T(128)}, f32[16,128,64]{2,1,0:T(8,128)S(1)}, f32[8,16,128,64]{3,2,1,0:T(8,128)}, f32[8,16]{1,0:T(8,128)S(1)}, f32[8,16,128,64]{2,3,1,0:T(8,128)}, /*index=5*/s32[]{:T(128)}, s32[]{:T(128)}) while((s32[]{:T(128)}, f32[16,128,64]{2,1,0:T(8,128)S(1)}, f32[8,16,128,64]{3,2,1,0:T(8,128)}, f32[8,16]{1,0:T(8,128)S(1)}, ...), condition=%wide.region_2.3_spmd.clone, body=%wide.region_1.2_spmd.clone.sunk | while | flops 524291 | bytes 5243680 | solution.py:35
  61.3 15.5 %all-reduce = f32[128]{0:T(128)S(1)} all-reduce(f32[128]{0:T(128)S(1)} %dynamic-update-slice), channel_id=2, replica_groups=mesh['ctx'=8,'exp'=4] {'ctx'}, use_global_device_ids=true, to_apply=%add | all-reduce | flops 128 | bytes 1024
  77.8 4.5 %reshape.93 = f32[8,128,16,64]{3,2,1,0:T(8,128)} reshape(bf16[1024,1024]{1,0:T(8,128)(2,1)S(1)} %copy-done.3) | data formatting | bytes 6291456 | tf_op jit(solution)/shard_map/reshape | solution.py:93
  82.3 7.2 %copy.94 = f32[8,128,16,64]{1,3,2,0:T(8,128)} copy(f32[8,128,16,64]{3,2,1,0:T(8,128)} %reshape.93) | data formatting | bytes 8388608 | tf_op jit(solution)/shard_map/reshape | solution.py:93
  89.6 2.5 mul.138
  92.0 5.4 %copy.90 = f32[1024,1024]{1,0:T(8,128)} copy(f32[1024,1024]{0,1:T(8,128)} %bitcast.98) | data formatting | bytes 8388608 | tf_op jit(solution)/shard_map/mul | solution.py:66
  98.0 12.5 %fusion.41 = f32[8,16,64,128]{3,2,1,0:T(8,128)} fusion(f32[8,16,128,64]{3,2,1,0:T(8,128)} %get-tuple-element.33, bf16[8,128,128,1]{2,1,3,0:T(8,128)(2,1)S(1)} %bitcast.95), kind=kOutput, calls=%fused_computation.70 | convolution fusion | flops 1610612736 | bytes 8650752 | tf_op jit(solution)/shard_map/bin,hbi,bhnp->bihp/dot_general | solution.py:38
  110.5 18.0 %fusion.2 = f32[8,16,64,128]{3,2,1,0:T(8,128)} fusion(f32[16,8,128]{2,0,1:T(8,128)S(1)} %copy_bitcast_fusion.2, f32[8,128,128]{2,1,0:T(8,128)S(1)} %fusion.40, f32[16,8,128]{2,0,1:T(8,128)S(1)} %copy.75, pred[128,128]{1,0:T(8,128)(4,1)S(1)} %iota_compare_fusion.3, f32[8,128,16,64]{1,3,2,0:T(8,128)S(1)} %copy-done.2, f32[8,16]{1,0:T(8,128)S(1)} %multiply_exponential_fusion), kind=kOutput, calls=%fused_computation.6 | convolution fusion | flops 1620049920 | bytes 9060864 | tf_op jit(solution)/shard_map/hbij,bjhp->bihp/dot_general | solution.py:24
  130.6 9.6 %multiply_reduce_fusion.1 = (f32[8,128,16]{1,2,0:T(8,128)S(1)}, f32[8,128,16,64]{1,3,2,0:T(8,128)}) fusion(f32[8,128,16,64]{1,3,2,0:T(8,128)} %copy.94, f32[8,128,16,64]{1,3,2,0:T(8,128)} %copy.74, f32[16]{0:T(128)S(1)} %copy-done.10, f32[8,16]{1,0:T(8,128)S(1)} %multiply_exponential_fusion, bf16[8,128,128,1]{2,1,3,0:T(8,128)(2,1)S(1)} %bitcast.96, ...), kind=kOutput, calls=%fused_computation.20 | convolution fusion | flops 1625276416 | bytes 21955136 | tf_op jit(solution)/shard_map/bin,hbi,hnp->bihp/dot_general | solution.py:88
  140.2 7.2 %copy.110 = f32[8,128,16,64]{3,2,1,0:T(8,128)} copy(f32[8,128,16,64]{1,3,2,0:T(8,128)} %get-tuple-element.89) | data formatting | bytes 8388608 | tf_op jit(solution)/shard_map/reshape | solution.py:89
  147.4 7.7 %reshape.92 = f32[1024,1024]{1,0:T(8,128)} reshape(f32[8,128,16,64]{3,2,1,0:T(8,128)} %copy.110) | data formatting | bytes 8388608 | tf_op jit(solution)/shard_map/reshape | solution.py:89
  155.1 2.5 mul.149
  157.6 5.4 %copy.96 = f32[1024,1024]{1,0:T(8,128)} copy(f32[1024,1024]{0,1:T(8,128)} %bitcast.99) | data formatting | bytes 8388608 | tf_op jit(solution)/shard_map/mul | solution.py:97
  163.0 7.0 %multiply_convert_fusion = bf16[1024,1024]{1,0:T(8,128)(2,1)S(1)} fusion(f32[1024,1024]{1,0:T(8,128)} %copy.96, f32[1024,1024]{1,0:T(8,128)} %reshape.92, f32[1024,1024]{1,0:T(8,128)} %copy.90, f32[1024]{0:T(1024)S(1)} %copy-done.9, f32[1024]{0:T(1024)S(1)} %mul.134, bf16[1024,1024]{1,0:T(8,128)(2,1)S(1)} %copy-done.3, bf16[1024,1024]{1,0:T(8,128)(2,1)} %param.15), kind=kLoop, calls=%fused_computation.19 | loop fusion | flops 13631488 | bytes 18882560 | tf_op jit(solution)/shard_map/convert_element_type | solution.py:99
  173.8 12.9 %collective-permute-done = bf16[256,1024]{1,0:T(8,128)(2,1)S(1)} collective-permute-done((bf16[256,1024]{1,0:T(8,128)(2,1)S(1)}, bf16[256,1024]{1,0:T(8,128)(2,1)S(1)}, u32[]{:S(2)}, u32[]{:S(2)}) %collective-permute-start) | collective-permute-done | bytes 524320 | tf_op jit(solution)/shard_map/ppermute | solution.py:108
  186.6 13.7 %collective-permute-done.1 = bf16[256,1024]{1,0:T(8,128)(2,1)S(1)} collective-permute-done((bf16[256,1024]{1,0:T(8,128)(2,1)S(1)}, bf16[256,1024]{1,0:T(8,128)(2,1)S(1)}, u32[]{:S(2)}, u32[]{:S(2)}) %collective-permute-start.1) | collective-permute-done | bytes 524320 | tf_op jit(solution)/shard_map/ppermute | solution.py:108
  200.3 12.8 %collective-permute-done.2 = bf16[256,1024]{1,0:T(8,128)(2,1)S(1)} collective-permute-done((bf16[256,1024]{1,0:T(8,128)(2,1)S(1)}, bf16[256,1024]{1,0:T(8,128)(2,1)S(1)}, u32[]{:S(2)}, u32[]{:S(2)}) %collective-permute-start.2) | collective-permute-done | bytes 524320 | tf_op jit(solution)/shard_map/ppermute | solution.py:108
  220.2 11.2 %convolution_convert_fusion = bf16[256,4096]{1,0:T(8,128)(2,1)} fusion(bf16[768,4096]{1,0:T(8,128)(2,1)} %all-gather.8.cloned.1.call-done, bf16[4096,768]{1,0:T(8,128)(2,1)} %all-gather.6.cloned.1.call-done, bf16[256,8192]{1,0:T(8,128)(2,1)} %constant_dynamic-update-slice_fusion, s32[]{:T(128)S(6)} %select_n.29), kind=kOutput, calls=%fused_computation.12 | convolution fusion | flops 3223257088 | bytes 16777220 | tf_op jit(solution)/shard_map/dot_general | solution.py:119
  231.5 44.6 %reduce-scatter.2.cloned.1.call-done = bf16[256,1024]{1,0:T(8,128)(2,1)} async-done(((bf16[256,4096]{1,0:T(8,128)(2,1)}), bf16[256,1024]{1,0:T(8,128)(2,1)}) %reduce-scatter.2.cloned.1.call-update) | async-done | bytes 524304 | tf_op jit(solution)/shard_map/reduce_scatter | solution.py:124
  276.0 3.3 %add_convert_fusion = bf16[1024,1024]{1,0:T(8,128)(2,1)} fusion(bf16[1024,1024]{1,0:T(8,128)(2,1)S(1)} %copy-done.5, bf16[256,1024]{1,0:T(8,128)(2,1)} %reduce-scatter.2.cloned.1.call-done, f32[1024]{0:T(1024)S(1)} %copy-done.12, s32[1024]{0:T(1024)S(1)} %copy-done.11), kind=kOutput, calls=%fused_computation.18 | convolution fusion | flops 541327360 | bytes 4726784 | tf_op jit(solution)/shard_map/dot_general | solution.py:128
  (127 shorter events, 43.4 us)
Async XLA Ops:
  6.5 91.2 %copy-start = (bf16[1024,128]{1,0:T(8,128)(2,1)S(1)}, bf16[1024,128]{1,0:T(8,128)(2,1)}, u32[]{:S(2)}) copy-start(bf16[1024,128]{1,0:T(8,128)(2,1)} %param.20) | copy-start | bytes 786436
  6.5 122.0 %all-gather.10.cloned.1.call-start = ((), (), s32[]{:S(2)}) async-start(), calls=%async_computation.4 | async-start | bytes 2359296 | tf_op jit(solution)/shard_map/all_gather | solution.py:78
  21.9 7.2 %copy-start.6 = (bf16[1024,128]{1,0:T(8,128)(2,1)S(1)}, bf16[1024,128]{1,0:T(8,128)(2,1)}, u32[]{:S(2)}) copy-start(bf16[1024,128]{1,0:T(8,128)(2,1)} %param.19) | copy-start | bytes 786436
  35.5 24.3 %copy-start.13 = (u32[32]{0:T(128)S(1)}, u32[32]{0:T(128)}, u32[]{:S(2)}) copy-start(u32[32]{0:T(128)} %constant.82) | copy-start | bytes 388
  57.3 20.5 %copy-start.3 = (bf16[1024,1024]{1,0:T(8,128)(2,1)S(1)}, bf16[1024,1024]{1,0:T(8,128)(2,1)}, u32[]{:S(2)}) copy-start(bf16[1024,1024]{1,0:T(8,128)(2,1)} %param.22) | copy-start | bytes 6291460
  58.2 162.0 %all-gather.6.cloned.1.call-start = ((), (), s32[]{:S(2)}) async-start(), calls=%async_computation.1 | async-start | bytes 7077888 | tf_op jit(solution)/shard_map/all_gather | solution.py:115
  59.0 161.2 %all-gather.8.cloned.1.call-start = ((), (), s32[]{:S(2)}) async-start(), calls=%async_computation.2 | async-start | bytes 7077888 | tf_op jit(solution)/shard_map/all_gather | solution.py:121
  59.7 216.3 %reduce-scatter.2.cloned.1.call-start = ((), (), s32[]{:S(2)}) async-start(), calls=%async_computation.3 | async-start | bytes 2621440 | tf_op jit(solution)/shard_map/reduce_scatter | solution.py:124
  92.0 5.4 %copy-start.10 = (f32[16]{0:T(128)S(1)}, f32[16]{0:T(128)}, u32[]{:S(2)}) copy-start(f32[16]{0:T(128)} %param.21) | copy-start | bytes 196
  92.0 5.7 %copy-start.8 = (f32[16,1024]{1,0:T(8,128)S(1)}, f32[16,1024]{1,0:T(8,128)}, u32[]{:S(2)}) copy-start(f32[16,1024]{1,0:T(8,128)} %param.17) | copy-start | bytes 196612
  92.0 5.7 %copy-start.7 = (bf16[1024,128]{1,0:T(8,128)(2,1)S(1)}, bf16[1024,128]{1,0:T(8,128)(2,1)}, u32[]{:S(2)}) copy-start(bf16[1024,128]{1,0:T(8,128)(2,1)} %param.19) | copy-start | bytes 786436
  98.0 12.5 %copy-start.2 = (f32[8,128,16,64]{1,3,2,0:T(8,128)S(1)}, f32[8,128,16,64]{1,3,2,0:T(8,128)}, u32[]{:S(2)}) copy-start(f32[8,128,16,64]{1,3,2,0:T(8,128)} %copy.74) | copy-start | bytes 12582916
  157.6 5.4 %copy-start.9 = (f32[1024]{0:T(1024)S(1)}, f32[1024]{0:T(1024)}, u32[]{:S(2)}) copy-start(f32[1024]{0:T(1024)} %param.23) | copy-start | bytes 12292
  163.0 8.3 %copy-start.11 = (s32[1024]{0:T(1024)S(1)}, s32[1024]{0:T(1024)}, u32[]{:S(2)}) copy-start(s32[1024]{0:T(1024)} %param.26) | copy-start | bytes 12292
  170.0 1.3 copy-start.4
  172.0 14.6 %collective-permute-start = (bf16[256,1024]{1,0:T(8,128)(2,1)S(1)}, bf16[256,1024]{1,0:T(8,128)(2,1)S(1)}, u32[]{:S(2)}, u32[]{:S(2)}) collective-permute-start(bf16[256,1024]{1,0:T(8,128)(2,1)S(1)} %convolution_convert_fusion.1), channel_id=1, source_target_pairs={{0,1},{1,2},{2,3},{3,0},{4,5},{5,6},{6,7},{7,4},{8,9},{9,10},{10,1... | collective-permute-start | bytes 1572872 | tf_op jit(solution)/shard_map/ppermute | solution.py:108
  186.6 13.7 %collective-permute-start.1 = (bf16[256,1024]{1,0:T(8,128)(2,1)S(1)}, bf16[256,1024]{1,0:T(8,128)(2,1)S(1)}, u32[]{:S(2)}, u32[]{:S(2)}) collective-permute-start(bf16[256,1024]{1,0:T(8,128)(2,1)S(1)} %collective-permute-done), channel_id=1, source_target_pairs={{0,1},{1,2},{2,3},{3,0},{4,5},{5,6},{6,7},{7,4},{8,9},{9,10},{10,1... | collective-permute-start | bytes 1572872 | tf_op jit(solution)/shard_map/ppermute | solution.py:108
  200.3 12.9 %collective-permute-start.2 = (bf16[256,1024]{1,0:T(8,128)(2,1)S(1)}, bf16[256,1024]{1,0:T(8,128)(2,1)S(1)}, u32[]{:S(2)}, u32[]{:S(2)}) collective-permute-start(bf16[256,1024]{1,0:T(8,128)(2,1)S(1)} %collective-permute-done.1), channel_id=1, source_target_pairs={{0,1},{1,2},{2,3},{3,0},{4,5},{5,6},{6,7},{7,4},{8,9},{9,10},{10,1... | collective-permute-start | bytes 1572872 | tf_op jit(solution)/shard_map/ppermute | solution.py:108
  220.2 55.9 %copy-start.5 = (bf16[1024,1024]{1,0:T(8,128)(2,1)S(1)}, bf16[1024,1024]{1,0:T(8,128)(2,1)}, u32[]{:S(2)}) copy-start(bf16[1024,1024]{1,0:T(8,128)(2,1)} %copy-done.4) | copy-start | bytes 6291460
  220.2 55.9 %copy-start.12 = (f32[1024]{0:T(1024)S(1)}, f32[1024]{0:T(1024)}, u32[]{:S(2)}) copy-start(f32[1024]{0:T(1024)} %param.27) | copy-start | bytes 12292
  220.2 59.1 %copy-start.1 = (bf16[1024,128]{1,0:T(8,128)(2,1)S(1)}, bf16[1024,128]{1,0:T(8,128)(2,1)}, u32[]{:S(2)}) copy-start(bf16[1024,128]{1,0:T(8,128)(2,1)} %param.20) | copy-start | bytes 786436
Sparse Core Ops, SparseCore 0:
  58.3 30.5 all-gather.9
  90.8 45.3 all-gather.5
  138.1 46.5 all-gather.7
  231.6 44.4 reduce-scatter.1
